TPU v7x, 32 devices: a whole 2x2x4 slice. The times are simulated.
32 devices in a mesh: rep: 2 (over x), seq: 8 (over z, y), head: 2 (over core).
Axes of the slice: x: 2, y: 2, z: 4, core: 2. Of those that a mesh axis runs over, the one named last changes fastest.
Arguments:
- query_rows: bfloat16 [2048, 4096], P(('rep', 'seq'), 'head'), parts along dimension 0, may hold values from -40 to 40
- key_rows: bfloat16 [2048, 4096], P(('rep', 'seq'), 'head'), parts along dimension 0, may hold values from -6 to 6
- value_rows: bfloat16 [2048, 4096], P(('rep', 'seq'), 'head'), parts along dimension 0, may hold values from -6 to 6
- rand_blocks: int32 [16, 32, 3], P('rep'), parts along dimension 0, may hold values from 0 to 7, as said below
- out_weight: bfloat16 [4096, 4096], P('seq', 'head'), may hold values from -0.09375 to 0.09375
Outputs:
- projected: bfloat16 [2048, 4096], P(('rep', 'seq'), 'head'), parts along dimension 0
There are 2 independent parts, one for each index of `rep`. A program takes and returns all parts, laid end to end along the dimension named above; an argument that names none is the same for every part. Nothing has to cross between parts.
Inputs may be any that keep to these rules, and one draw needn't show every extreme that they name: `rand_blocks`: each entry is uniform over the blocks of the whole sequence. For the query blocks of one index of seq and the heads of one index of head, at most 6 entries name blocks held by one index of seq, and in every draw some index of seq is named exactly 6 times.
All inputs are finite; a program needn't handle non-finite values.
Results may differ from a plain program's by a relative error of at most 0.008.
Values may be sent and summed in bfloat16 or wider, within the bound.
No kernel may reach another device: no remote copies, remote signals or barrier semaphores. Data moves between devices by JAX's collectives and lax.ppermute only.
A program may use at most 128 MiB of HBM per device.

v0:
```python
import math
import jax
import jax.numpy as jnp
from jax import lax
from jax.sharding import PartitionSpec as P

HD = 128
BLK = 128
R = 3


def broadcast(block, axis, owner):
    block = jnp.where(lax.axis_index(axis) == owner, block, jnp.zeros_like(block))
    return lax.psum(block, axis)


def padded(array, sides, width):
    for axis, dim in sides:
        peers, length = (lax.axis_size(axis), array.shape[dim])
        up = [(i, (i + 1) % peers) for i in range(peers - 1)]
        down = [(j, i) for i, j in up]
        last = lax.slice_in_dim(array, length - width, length, axis=dim)
        initial = lax.slice_in_dim(array, 0, width, axis=dim)
        before = lax.ppermute(last, axis, up)
        after = lax.ppermute(initial, axis, down)
        array = jnp.concatenate([before, array, after], axis=dim)
    return array


def masked_softmax(scores, allowed):
    masked = jnp.where(allowed, scores, -jnp.inf)
    row_peak = jnp.max(masked, axis=-1, keepdims=True)
    expon_terms = jnp.where(allowed, jnp.exp(masked - row_peak), 0.0)
    return expon_terms / jnp.sum(expon_terms, axis=-1, keepdims=True)


def share_block(stacked, root_index):
    return broadcast(stacked, "seq", root_index)


def local(query_rows, key_rows, value_rows, rand_blocks, out_weight):
    tokens, features = query_rows.shape
    head_width = HD
    head_count = features // head_width
    blocks = tokens // BLK
    seq_count = lax.axis_size("seq")
    seq_index = lax.axis_index("seq")
    head_index = lax.axis_index("head")
    block_total = blocks * seq_count
    score_scale = 1.0 / math.sqrt(head_width)
    request_count = blocks * head_count * R
    slot_depth = (request_count + seq_count - 1) // seq_count
    first_rows = jnp.stack((query_rows, key_rows, value_rows))
    final_rows = jnp.stack((query_rows, key_rows, value_rows))
    first_glob = share_block(first_rows, 0)
    final_glob = share_block(final_rows, seq_count - 1)
    paired = jnp.stack((key_rows, value_rows))
    extended = padded(paired, (("seq", 1),), BLK)
    ext_heads = extended.reshape(2, blocks + 2, BLK, head_count, head_width).transpose(
        0, 3, 1, 2, 4
    )
    group_table = lax.dynamic_slice_in_dim(rand_blocks, head_index * head_count, head_count, 1)
    all_requests = group_table.reshape(seq_count, request_count)
    all_owner = all_requests // blocks
    request_order = jnp.arange(request_count, dtype=jnp.int32)
    earlier_request = request_order[None, :] < request_order[:, None]
    same_owner = all_owner[:, :, None] == all_owner[:, None, :]
    all_position = jnp.sum(same_owner & earlier_request[None], axis=2)
    owned_here = all_owner == seq_index
    slot_range = jnp.arange(slot_depth, dtype=jnp.int32)
    picked = owned_here[:, None, :] & (all_position[:, None, :] == slot_range[None, :, None])
    picked_request = jnp.sum(jnp.where(picked, request_order[None, None, :], 0), axis=2)
    picked_block = jnp.take_along_axis(all_requests, picked_request, axis=1) - seq_index * blocks
    picked_block = jnp.clip(picked_block, 0, blocks - 1).reshape(-1)
    picked_head = (picked_request // R % head_count).reshape(-1)
    local_pairs = paired.reshape(2, blocks, BLK, head_count, head_width)
    outgoing = local_pairs[:, picked_block, :, picked_head, :]
    outgoing = outgoing.reshape(seq_count, slot_depth, 2, BLK, head_width)
    received = lax.all_to_all(outgoing, "seq", split_axis=0, concat_axis=0, tiled=True)
    my_requests = lax.dynamic_slice_in_dim(all_requests, seq_index, 1, 0)[0]
    my_position = lax.dynamic_slice_in_dim(all_position, seq_index, 1, 0)[0]
    my_owner = my_requests // blocks
    rand_pairs = jnp.take(
        received.reshape(seq_count * slot_depth, 2, BLK, head_width),
        my_owner * slot_depth + my_position,
        axis=0,
    )
    rand_pairs = rand_pairs.reshape(blocks, head_count, R, 2, BLK, head_width).transpose(
        3, 1, 0, 2, 4, 5
    )
    block_ids = seq_index * blocks + jnp.arange(blocks, dtype=jnp.int32)
    base_slots = jnp.stack(
        [
            jnp.zeros((blocks,), jnp.int32),
            jnp.full((blocks,), block_total - 1, jnp.int32),
            jnp.clip(block_ids - 1, 0, block_total - 1),
            block_ids,
            jnp.clip(block_ids + 1, 0, block_total - 1),
        ],
        axis=1,
    )
    my_table = my_requests.reshape(blocks, head_count, R).transpose(1, 0, 2)
    slot_ids = jnp.concatenate(
        [jnp.broadcast_to(base_slots[None], (head_count, blocks, 5)), my_table], axis=2
    )
    slot_count = slot_ids.shape[2]
    equal_pair = slot_ids[:, :, :, None] == slot_ids[:, :, None, :]
    earlier = jnp.arange(slot_count)[None, :] < jnp.arange(slot_count)[:, None]
    slot_live = jnp.logical_not(jnp.any(equal_pair & earlier[None, None], axis=3))
    key_live = jnp.repeat(slot_live, BLK, axis=2)
    window_index = jnp.arange(blocks)[:, None] + jnp.arange(3)[None, :]
    query_heads = query_rows.reshape(blocks, BLK, head_count, head_width).transpose(2, 0, 1, 3)
    first_heads = first_glob.reshape(3, BLK, head_count, head_width).transpose(0, 2, 1, 3)
    final_heads = final_glob.reshape(3, BLK, head_count, head_width).transpose(0, 2, 1, 3)
    target_heads = max(1, 512 // (blocks * BLK))
    heads_step = max(
        (
            width
            for width in range(1, head_count + 1)
            if head_count % width == 0 and width <= target_heads
        )
    )

    def collect(ext_part, first_block, final_block, rand_part):
        steps_here = ext_part.shape[0]
        window_blocks = ext_part[:, window_index]
        glob_blocks = jnp.stack((first_block, final_block), axis=1)[:, None]
        joined = jnp.concatenate([glob_blocks, window_blocks, rand_part], axis=2)
        return joined.reshape(steps_here, blocks, slot_count * BLK, head_width)

    def attend(head_items):
        (
            query_one,
            key_ext,
            value_ext,
            key_first,
            value_first,
            key_final,
            value_final,
            key_rand,
            value_rand,
            live_one,
        ) = head_items
        keys_sel = collect(key_ext, key_first, key_final, key_rand)
        values_sel = collect(value_ext, value_first, value_final, value_rand)
        scores = (
            jnp.einsum("hibd,hikd->hibk", query_one, keys_sel, preferred_element_type=jnp.float32)
            * score_scale
        )
        weights = masked_softmax(scores, live_one[:, :, None, :]).astype(jnp.bfloat16)
        mixed = jnp.einsum(
            "hibk,hikd->hibd", weights, values_sel, preferred_element_type=jnp.float32
        )
        return mixed.astype(jnp.bfloat16)

    def split_heads(array):
        return array.reshape((head_count // heads_step, heads_step) + array.shape[1:])

    head_inputs = (
        query_heads,
        ext_heads[0],
        ext_heads[1],
        first_heads[1],
        first_heads[2],
        final_heads[1],
        final_heads[2],
        rand_pairs[0],
        rand_pairs[1],
        key_live,
    )
    block_heads = lax.map(attend, tuple((split_heads(item) for item in head_inputs)))
    block_heads = block_heads.reshape(head_count, blocks, BLK, head_width)
    attended = block_heads.transpose(1, 2, 0, 3).reshape(tokens, features)
    glob_query = jnp.concatenate((first_glob[0], final_glob[0]), axis=0).reshape(
        2 * BLK, head_count, head_width
    )
    key_heads = key_rows.reshape(tokens, head_count, head_width)
    value_wide = value_rows.reshape(tokens, head_count, head_width).astype(jnp.float32)
    glob_scores = (
        jnp.einsum("rhd,thd->hrt", glob_query, key_heads, preferred_element_type=jnp.float32)
        * score_scale
    )
    local_peak = jnp.max(glob_scores, axis=2)
    row_peak = lax.pmax(local_peak, "seq")
    expon_terms = jnp.exp(glob_scores - row_peak[:, :, None])
    denoms = jnp.sum(expon_terms, axis=2)
    numer_terms = jnp.einsum(
        "hrt,thd->hrd", expon_terms, value_wide, preferred_element_type=jnp.float32
    )
    numer_terms, denoms = lax.psum((numer_terms, denoms), "seq")
    glob_out = (
        (numer_terms / denoms[:, :, None])
        .astype(jnp.bfloat16)
        .transpose(1, 0, 2)
        .reshape(2 * BLK, features)
    )
    head_block = jnp.where(seq_index == 0, glob_out[:BLK], attended)
    attended = attended.at[:BLK].set(head_block)
    tail_block = jnp.where(seq_index == seq_count - 1, glob_out[BLK:], attended)
    attended = attended.at[tokens - BLK :].set(tail_block)
    partial_terms = lax.dot_general(
        lax.all_gather(out_weight, "seq", axis=0, tiled=True),
        attended,
        (((1,), (1,)), ((), ())),
        preferred_element_type=jnp.float32,
    )
    summed = lax.psum_scatter(
        partial_terms.astype(jnp.bfloat16), "head", scatter_dimension=0, tiled=True
    ).astype(jnp.float32)
    return summed.T.astype(jnp.bfloat16)


def solution(mesh):
    placed = (
        P(("rep", "seq"), "head"),
        P(("rep", "seq"), "head"),
        P(("rep", "seq"), "head"),
        P("rep", None, None),
        P("seq", "head"),
    )
    return jax.shard_map(
        local, mesh=mesh, in_specs=placed, out_specs=P(("rep", "seq"), "head"), check_vma=False
    )
```

profile of v0, /device:TPU:0, one launch (start us, length us, event | category | flops | bytes accessed | tf_op | source)
XLA Modules:
  0.0 597.0 jit_solution(8939532959045065275)
XLA Ops:
  7.9 1.5 copy.85
  9.7 1.9 broadcast_select_fusion
  11.8 132.2 %all-reduce.6.cloned.1.call-done = (bf16[3,128,2048]{1,2,0:T(8,128)(2,1)}, bf16[3,128,2048]{1,2,0:T(8,128)(2,1)}) async-done(((bf16[3,128,2048]{1,2,0:T(8,128)(2,1)}, bf16[3,128,2048]{1,2,0:T(8,128)(2,1)}), (bf16[3,128,2048]{1,2,0:T(8,128)(2,1)}, bf16[3,128,2048]{1,2,0:T(8,128)(2,1)})) %all-reduce.6.cloned.1.call-update) | async-done | bytes 3145744 | tf_op jit(solution)/shard_map/psum | solution.py:14
  148.2 1.8 multiply_reduce_fusion
  150.0 35.1 %pmax.7 = f32[16,256]{1,0:T(8,128)S(1)} all-reduce(f32[16,256]{1,0:T(8,128)S(1)} %get-tuple-element.247), channel_id=1, replica_groups=mesh['rep'=2,'seq'=8,'head'=2] {'seq'}, use_global_device_ids=true, to_apply=%region_3.4 | all-reduce | flops 4096 | bytes 32768 | tf_op jit(solution)/shard_map/pmax | solution.py:184
  185.1 3.0 fusion.25
  194.4 2.8 gather_fusion.2
  197.2 4.6 all-to-all-start
  202.9 4.7 collective-permute-start
  213.0 35.9 %collective-permute-done = bf16[2,128,2048]{1,2,0:T(8,128)(2,1)} collective-permute-done((bf16[2,128,2048]{1,2,0:T(8,128)(2,1)}, bf16[2,128,2048]{1,2,0:T(8,128)(2,1)}, u32[]{:S(2)}, u32[]{:S(2)}) %collective-permute-start) | collective-permute-done | bytes 1048608 | tf_op jit(solution)/shard_map/ppermute | solution.py:24
  248.8 3.3 pad_maximum_fusion.2
  252.1 4.7 copy.100
  256.8 2.9 copy.128
  259.8 2.2 fusion.58
  263.1 2.1 fusion.59
  265.2 2.1 copy.99
  269.7 101.5 %psum.31 = f32[16,256]{1,0:T(8,128)S(1)} all-reduce(f32[16,256]{1,0:T(8,128)S(1)} %fusion.24), channel_id=1, replica_groups=mesh['rep'=2,'seq'=8,'head'=2] {'seq'}, use_global_device_ids=true, to_apply=%region_6.7 | all-reduce | flops 4096 | bytes 32768 | tf_op jit(solution)/shard_map/psum | solution.py:190
  371.2 1.9 fusion.32
  375.4 3.1 gather_fusion.3
  378.8 1.5 fusion.57
  380.3 49.2 %while.16 = (s32[]{:T(128)}, bf16[4,4,1,128,128]{3,4,1,0,2:T(8,128)(2,1)}, pred[4,4,1,1024]{3,1,2,0:T(4,128)(4,1)S(1)}, bf16[4,4,1,128,128]{4,3,1,2,0:T(8,128)(2...) while((s32[]{:T(128)}, ...), condition=%wide.region_13.14_spmd.clone.clone, body=%wide.region_10.13_spmd.clone.clone.sunk | while | flops 274532352 | bytes 33842396 | solution.py:171
  381.3 1.4 constant_dynamic-slice_fusion.10
  384.8 3.1 fusion.76
  393.6 1.4 constant_dynamic-slice_fusion.10
  397.1 3.1 fusion.76
  405.9 1.4 constant_dynamic-slice_fusion.10
  409.4 3.1 fusion.76
  421.7 3.1 fusion.76
  429.5 1.9 fusion.37
  431.4 139.7 %all-gather.2.cloned.1.call-done = bf16[4096,2048]{1,0:T(8,128)(2,1)} async-done(((bf16[512,2048]{1,0:T(8,128)(2,1)}), bf16[4096,2048]{1,0:T(8,128)(2,1)}) %all-gather.2.cloned.1.call-update) | async-done | bytes 16777232 | tf_op jit(solution)/shard_map/all_gather | solution.py:202
  571.1 12.5 %fusion.22 = bf16[4096,128]{0,1:T(8,128)(2,1)} fusion(bf16[128,2048]{0,1:T(8,128)(2,1)S(1)} %fusion.37, bf16[4096,2048]{1,0:T(8,128)(2,1)} %all-gather.2.cloned.1.call-done), kind=kOutput, calls=%fused_computation.43 | convolution fusion | flops 2148007936 | bytes 18350080 | tf_op jit(solution)/shard_map/dot_general | solution.py:201
  583.6 6.9 %reduce-scatter.2.cloned.1.call-done = bf16[2048,128]{0,1:T(8,128)(2,1)} async-done(((bf16[4096,128]{0,1:T(8,128)(2,1)}), bf16[2048,128]{0,1:T(8,128)(2,1)}) %reduce-scatter.2.cloned.1.call-update) | async-done | bytes 524304 | tf_op jit(solution)/shard_map/reduce_scatter | solution.py:207
  (175 shorter events, 56.7 us)
Async XLA Ops:
  6.5 182.3 %copy-start = (s32[8,32,3]{1,0,2:T(8,128)S(1)}, s32[8,32,3]{1,0,2:T(8,128)}, u32[]{:S(2)}) copy-start(s32[8,32,3]{1,0,2:T(8,128)} %param.18) | copy-start | bytes 9220
  6.5 2.9 copy-start.6
  6.5 137.5 %all-reduce.6.cloned.1.call-start = ((), (), s32[]{:S(2)}) async-start(), calls=%async_computation.5 | async-start | bytes 6291456 | tf_op jit(solution)/shard_map/psum | solution.py:14
  7.9 183.0 %copy-start.2 = (bf16[128,2048]{0,1:T(8,128)(2,1)}, bf16[128,2048]{0,1:T(8,128)(2,1)S(1)}, u32[]{:S(2)}) copy-start(bf16[128,2048]{0,1:T(8,128)(2,1)S(1)} %copy.84) | copy-start | bytes 1572868
  9.4 182.5 %copy-start.4 = (bf16[128,2048]{0,1:T(8,128)(2,1)}, bf16[128,2048]{0,1:T(8,128)(2,1)S(1)}, u32[]{:S(2)}) copy-start(bf16[128,2048]{0,1:T(8,128)(2,1)S(1)} %copy.85) | copy-start | bytes 1572868
  11.7 359.5 %all-reduce.4.cloned.1.call-start = ((), (), s32[]{:S(2)}) async-start(), calls=%async_computation.2 | async-start | bytes 4194304 | tf_op jit(solution)/shard_map/psum | solution.py:190
  188.1 382.9 %all-gather.2.cloned.1.call-start = ((), (), s32[]{:S(2)}) async-start(), calls=%async_computation.3 | async-start | bytes 18874368 | tf_op jit(solution)/shard_map/all_gather | solution.py:202
  197.2 4.6 copy-start.3
  197.2 4.6 copy-start.5
  197.2 178.2 %all-to-all-start = ((bf16[8,6,2,128,128]{4,3,2,1,0:T(8,128)(2,1)}), bf16[8,6,2,128,128]{4,3,2,1,0:T(8,128)(2,1)}, u32[]{:S(2)}, u32[]{:S(2)}) async-start(bf16[8,6,2,128,128]{4,3,2,1,0:T(8,128)(2,1)} %bitcast.194), calls=%async_computation | async-start | bytes 6291456 | tf_op jit(solution)/shard_map/all_to_all | solution.py:79
  201.7 388.7 %reduce-scatter.2.cloned.1.call-start = ((), (), s32[]{:S(2)}) async-start(), calls=%async_computation.4 | async-start | bytes 1572864 | tf_op jit(solution)/shard_map/reduce_scatter | solution.py:207
  202.9 45.9 %collective-permute-start = (bf16[2,128,2048]{1,2,0:T(8,128)(2,1)}, bf16[2,128,2048]{1,2,0:T(8,128)(2,1)}, u32[]{:S(2)}, u32[]{:S(2)}) collective-permute-start(bf16[2,128,2048]{1,2,0:T(8,128)(2,1)} %pad_maximum_fusion.4), channel_id=1, source_target_pairs={{0,2},{2,4},{4,6},{6,8},{8,10},{10,12},{12,14},{1,3},{3,5},{5,7},{... | collective-permute-start | bytes 3145736 | tf_op jit(solution)/shard_map/ppermute | solution.py:24
  207.6 41.2 %collective-permute-start.1 = (bf16[2,128,2048]{1,2,0:T(8,128)(2,1)}, bf16[2,128,2048]{1,2,0:T(8,128)(2,1)}, u32[]{:S(2)}, u32[]{:S(2)}) collective-permute-start(bf16[2,128,2048]{1,2,0:T(8,128)(2,1)} %pad_maximum_fusion.4), channel_id=1, source_target_pairs={{2,0},{4,2},{6,4},{8,6},{10,8},{12,10},{14,12},{3,1},{5,3},{7,5},{... | collective-permute-start | bytes 3145736 | tf_op jit(solution)/shard_map/ppermute | solution.py:25
  259.7 2.3 copy-start.7
  389.7 1.6 copy-start.8
  402.0 1.6 copy-start.8
  414.3 1.6 copy-start.8
  426.6 1.6 copy-start.8
  571.1 19.4 %copy-start.1 = (s32[8,32,3]{1,0,2:T(8,128)S(1)}, s32[8,32,3]{1,0,2:T(8,128)}, u32[]{:S(2)}) copy-start(s32[8,32,3]{1,0,2:T(8,128)} %param.18) | copy-start | bytes 9220
Sparse Core Ops, SparseCore 0:
  11.8 132.1 all-reduce.5
  188.3 152.7 all-reduce.3
  343.4 227.6 all-gather.1
  583.7 6.7 reduce-scatter.1
where the time goes:
time: 599 us; the launch traced here: 597 us
  waiting for transfers between devices  315 us (53%)
  blocking collectives  137 us (23%)
  local copies, waits for them, and re-layouts  73.9 us (12%)
  matrix products  31.6 us (5%)
  other arithmetic  14.8 us (2%)
  between operations  13.4 us (2%)
  starting transfers between devices  10.7 us (2%)
    all_gather x1, waiting for transfers between devices, local(): lax.all_gather(out_weight, 'seq', axis=0, tiled=True)  140 us
    psum x1, waiting for transfers between devices, broadcast(): return lax.psum(block, axis)  132 us
    psum x1, blocking collectives, local(): numer_terms, denoms = lax.psum((numer_terms, denoms), 'seq')  102 us
    ppermute x1, waiting for transfers between devices, padded(): before = lax.ppermute(last, axis, up)  35.9 us
    pmax x1, blocking collectives, local(): row_peak = lax.pmax(local_peak, 'seq')  35.1 us
    dot_general x1, matrix products, local(): lax.dot_general(lax.all_gather(out_weight, 'seq', axis=0, tiled=True), at...  12.5 us
    sub x4, matrix products, masked_softmax(): expon_terms = jnp.where(allowed, jnp.exp(masked - row_peak), 0.0)  12.3 us
  transfers between devices with their start and end apart: 7, of which 4 were waited for; matrix products, arithmetic and copies ran while one was open for 15% of the time, Pallas kernels for 0%

commit v1 on v0

--- a/solution.py
+++ b/solution.py
@@ -11,7 +11,7 @@
 
 def broadcast(block, axis, owner):
     block = jnp.where(lax.axis_index(axis) == owner, block, jnp.zeros_like(block))
-    return lax.psum(block, axis)
+    return jnp.sum(lax.all_gather(block, axis), axis=0)
 
 
 def padded(array, sides, width):

time: 599 us -> 825 us (1.38)
  waiting for transfers between devices: 315 us -> 574 us
  blocking collectives: 137 us -> 98.7 us
  other arithmetic: 14.8 us -> 31.7 us
  local copies, waits for them, and re-layouts: 73.9 us -> 64.4 us
    all_gather x0 -> x2, waiting for transfers between devices: none -> 346 us  [broadcast(): return jnp.sum(lax.all_gather(block, axis), axis=0)]
    psum x1 -> x0, waiting for transfers between devices: 132 us -> none  [broadcast(): return lax.psum(block, axis)]
    psum x1, blocking collectives: 102 us -> 64.5 us  [local(): numer_terms, denoms = lax.psum((numer_terms, denoms), 'seq')]
    all_to_all x1, waiting for transfers between devices: 0.01 us -> 36 us  [local(): lax.all_to_all(outgoing, 'seq', split_axis=0, concat_axis=0, tiled=True)]
    reduce_sum x0 -> x2, other arithmetic: none -> 16.9 us  [broadcast(): return jnp.sum(lax.all_gather(block, axis), axis=0)]
    all_gather x1, waiting for transfers between devices: 140 us -> 148 us  [local(): lax.all_gather(out_weight, 'seq', axis=0, tiled=True)]
  transfers between devices with their start and end apart: 7 -> 8, of which waited for: 4 -> 6; matrix products, arithmetic and copies ran while one was open for 15% -> 11% of each run, Pallas kernels for 0% -> 0%
where the time goes in v1:
time: 825 us; the launch traced here: 824 us
  waiting for transfers between devices  574 us (70%)
  blocking collectives  98.7 us (12%)
  local copies, waits for them, and re-layouts  64.4 us (8%)
  other arithmetic  31.7 us (4%)
  matrix products  30.5 us (4%)
  between operations  13.4 us (2%)
  starting transfers between devices  10.9 us (1%)
    all_gather x2, waiting for transfers between devices, broadcast(): return jnp.sum(lax.all_gather(block, axis), axis=0)  346 us
    all_gather x1, waiting for transfers between devices, local(): lax.all_gather(out_weight, 'seq', axis=0, tiled=True)  148 us
    psum x1, blocking collectives, local(): numer_terms, denoms = lax.psum((numer_terms, denoms), 'seq')  64.5 us
    all_to_all x1, waiting for transfers between devices, local(): lax.all_to_all(outgoing, 'seq', split_axis=0, concat_axis=0, tiled=True)  36 us
    ppermute x1, waiting for transfers between devices, padded(): before = lax.ppermute(last, axis, up)  35.2 us
    pmax x1, blocking collectives, local(): row_peak = lax.pmax(local_peak, 'seq')  34.2 us
    reduce_sum x2, other arithmetic, broadcast(): return jnp.sum(lax.all_gather(block, axis), axis=0)  16.9 us
  transfers between devices with their start and end apart: 8, of which 6 were waited for; matrix products, arithmetic and copies ran while one was open for 11% of the time, Pallas kernels for 0%

profile of v1, /device:TPU:0, one launch (start us, length us, event | category | flops | bytes accessed | tf_op | source)
XLA Modules:
  0.0 823.8 jit_solution(16979699112830433158)
XLA Ops:
  6.5 3.4 broadcast_select_fusion
  10.8 178.5 %all-gather.4.cloned.1.call-done = bf16[8,3,128,2048]{3,2,1,0:T(8,128)(2,1)} async-done(((bf16[1,3,128,2048]{3,2,1,0:T(8,128)(2,1)}), bf16[8,3,128,2048]{3,2,1,0:T(8,128)(2,1)}) %all-gather.4.cloned.1.call-update) | async-done | bytes 12582928 | tf_op jit(solution)/shard_map/all_gather | solution.py:14
  189.3 7.7 reduce_sum.64
  198.3 167.8 %all-gather.6.cloned.1.call-done = bf16[8,3,128,2048]{3,2,1,0:T(8,128)(2,1)} async-done(((bf16[1,3,128,2048]{3,2,1,0:T(8,128)(2,1)}), bf16[8,3,128,2048]{3,2,1,0:T(8,128)(2,1)}) %all-gather.6.cloned.1.call-update) | async-done | bytes 12582928 | tf_op jit(solution)/shard_map/all_gather | solution.py:14
  366.1 9.2 %reduce_sum.65 = bf16[3,128,2048]{2,1,0:T(8,128)(2,1)} reduce(bf16[8,3,128,2048]{3,2,1,0:T(8,128)(2,1)} %all-gather.6.cloned.1.call-done, bf16[]{:T(256)} %constant.208.clone.1), dimensions={0}, to_apply=%region_1.2 | reduce | flops 5505024 | bytes 14155778 | tf_op jit(solution)/shard_map/reduce_sum | solution.py:14
  377.7 1.7 multiply_reduce_fusion
  379.4 34.2 %pmax.7 = f32[16,256]{1,0:T(8,128)S(1)} all-reduce(f32[16,256]{1,0:T(8,128)S(1)} %get-tuple-element.269), channel_id=1, replica_groups=mesh['rep'=2,'seq'=8,'head'=2] {'seq'}, use_global_device_ids=true, to_apply=%region_3.4 | all-reduce | flops 4096 | bytes 32768 | tf_op jit(solution)/shard_map/pmax | solution.py:184
  413.6 2.0 fusion.25
  423.7 2.8 gather_fusion.2
  426.5 4.6 all-to-all-start
  432.2 4.7 collective-permute-start
  442.3 35.2 %collective-permute-done = bf16[2,128,2048]{2,1,0:T(8,128)(2,1)} collective-permute-done((bf16[2,128,2048]{2,1,0:T(8,128)(2,1)}, bf16[2,128,2048]{2,1,0:T(8,128)(2,1)}, u32[]{:S(2)}, u32[]{:S(2)}) %collective-permute-start) | collective-permute-done | bytes 1048608 | tf_op jit(solution)/shard_map/ppermute | solution.py:24
  477.6 1.8 pad_maximum_fusion.2
  481.2 2.0 fusion.58
  483.2 36.0 %all-to-all-done = bf16[8,6,2,128,128]{4,3,2,1,0:T(8,128)(2,1)} async-done(((bf16[8,6,2,128,128]{4,3,2,1,0:T(8,128)(2,1)}), bf16[8,6,2,128,128]{4,3,2,1,0:T(8,128)(2,1)}, u32[]{:S(2)}, u32[]{:S(2)}) %all-to-all-start) | async-done | bytes 3145760 | tf_op jit(solution)/shard_map/all_to_all | solution.py:79
  519.2 4.7 gather_fusion.3
  524.0 2.2 fusion.23
  526.2 1.9 fusion.57
  528.1 2.6 copy.121
  530.7 2.6 copy.122
  533.7 64.5 %psum.15 = f32[16,256]{1,0:T(8,128)S(1)} all-reduce(f32[16,256]{1,0:T(8,128)S(1)} %fusion.24), channel_id=1, replica_groups=mesh['rep'=2,'seq'=8,'head'=2] {'seq'}, use_global_device_ids=true, to_apply=%region_6.7 | all-reduce | flops 4096 | bytes 32768 | tf_op jit(solution)/shard_map/psum | solution.py:190
  600.4 46.2 %while.16 = (s32[]{:T(128)}, bf16[4,4,1,128,128]{3,4,1,0,2:T(8,128)(2,1)}, pred[4,4,1,1024]{3,1,2,0:T(4,128)(4,1)S(1)}, bf16[4,4,1,128,128]{4,3,1,2,0:T(8,128)(2...) while((s32[]{:T(128)}, ...), condition=%wide.region_13.14_spmd.clone.clone, body=%wide.region_10.13_spmd.clone.clone.sunk | while | flops 274532352 | bytes 33318108 | solution.py:171
  605.0 3.1 fusion.76
  609.3 1.4 copy-done.11
  616.6 3.1 fusion.76
  620.8 1.4 copy-done.11
  628.1 3.1 fusion.76
  639.6 3.1 fusion.76
  646.6 1.9 fusion.32
  649.8 148.1 %all-gather.8.cloned.1.call-done = bf16[4096,2048]{1,0:T(8,128)(2,1)} async-done(((bf16[512,2048]{1,0:T(8,128)(2,1)}), bf16[4096,2048]{1,0:T(8,128)(2,1)}) %all-gather.8.cloned.1.call-update) | async-done | bytes 16777232 | tf_op jit(solution)/shard_map/all_gather | solution.py:202
  797.9 12.5 %fusion.22 = bf16[4096,128]{0,1:T(8,128)(2,1)} fusion(bf16[128,2048]{0,1:T(8,128)(2,1)S(1)} %fusion.37, bf16[4096,2048]{1,0:T(8,128)(2,1)} %all-gather.8.cloned.1.call-done), kind=kOutput, calls=%fused_computation.41 | convolution fusion | flops 2148007936 | bytes 18350080 | tf_op jit(solution)/shard_map/dot_general | solution.py:201
  810.4 6.9 reduce-scatter.2.cloned.1.call-done
  (193 shorter events, 55.1 us)
Async XLA Ops:
  6.5 411.7 %copy-start = (s32[8,32,3]{1,0,2:T(8,128)S(1)}, s32[8,32,3]{1,0,2:T(8,128)}, u32[]{:S(2)}) copy-start(s32[8,32,3]{1,0,2:T(8,128)} %param.18) | copy-start | bytes 9220
  6.5 182.7 %all-gather.4.cloned.1.call-start = ((), (), s32[]{:S(2)}) async-start(), calls=%async_computation.2 | async-start | bytes 14155776 | tf_op jit(solution)/shard_map/all_gather | solution.py:14
  10.0 356.1 %all-gather.6.cloned.1.call-start = ((), (), s32[]{:S(2)}) async-start(), calls=%async_computation.3 | async-start | bytes 14155776 | tf_op jit(solution)/shard_map/all_gather | solution.py:14
  10.7 635.9 %all-reduce.2.cloned.1.call-start = ((), (), s32[]{:S(2)}) async-start(), calls=%async_computation.4 | async-start | bytes 4194304 | tf_op jit(solution)/shard_map/psum | solution.py:190
  197.0 178.3 %copy-start.6 = (bf16[3,128,2048]{2,1,0:T(8,128)(2,1)}, bf16[3,128,2048]{2,1,0:T(8,128)(2,1)S(1)}, u32[]{:S(2)}) copy-start(bf16[3,128,2048]{2,1,0:T(8,128)(2,1)S(1)} %reduce_sum.64) | copy-start | bytes 4718596
  375.3 2.5 copy-start.4
  377.7 35.9 %copy-start.2 = (bf16[128,2048]{1,0:T(8,128)(2,1)S(1)}, bf16[128,2048]{1,0:T(8,128)(2,1)}, u32[]{:S(2)}) copy-start(bf16[128,2048]{1,0:T(8,128)(2,1)} %param.17) | copy-start | bytes 1572868
  415.6 382.3 %all-gather.8.cloned.1.call-start = ((), (), s32[]{:S(2)}) async-start(), calls=%async_computation.5 | async-start | bytes 18874368 | tf_op jit(solution)/shard_map/all_gather | solution.py:202
  419.3 1.1 copy-start.9
  419.3 2.1 copy-start.8
  426.5 4.6 copy-start.3
  426.5 4.6 copy-start.5
  426.5 92.7 %all-to-all-start = ((bf16[8,6,2,128,128]{4,3,2,1,0:T(8,128)(2,1)}), bf16[8,6,2,128,128]{4,3,2,1,0:T(8,128)(2,1)}, u32[]{:S(2)}, u32[]{:S(2)}) async-start(bf16[8,6,2,128,128]{4,3,2,1,0:T(8,128)(2,1)} %bitcast.193), calls=%async_computation | async-start | bytes 6291456 | tf_op jit(solution)/shard_map/all_to_all | solution.py:79
  431.1 386.2 %reduce-scatter.2.cloned.1.call-start = ((), (), s32[]{:S(2)}) async-start(), calls=%async_computation.6 | async-start | bytes 1572864 | tf_op jit(solution)/shard_map/reduce_scatter | solution.py:207
  432.2 45.3 %collective-permute-start = (bf16[2,128,2048]{2,1,0:T(8,128)(2,1)}, bf16[2,128,2048]{2,1,0:T(8,128)(2,1)}, u32[]{:S(2)}, u32[]{:S(2)}) collective-permute-start(bf16[2,128,2048]{2,1,0:T(8,128)(2,1)} %pad_maximum_fusion.4), channel_id=1, source_target_pairs={{0,2},{2,4},{4,6},{6,8},{8,10},{10,12},{12,14},{1,3},{3,5},{5,7},{... | collective-permute-start | bytes 3145736 | tf_op jit(solution)/shard_map/ppermute | solution.py:24
  437.0 40.6 %collective-permute-start.1 = (bf16[2,128,2048]{2,1,0:T(8,128)(2,1)}, bf16[2,128,2048]{2,1,0:T(8,128)(2,1)}, u32[]{:S(2)}, u32[]{:S(2)}) collective-permute-start(bf16[2,128,2048]{2,1,0:T(8,128)(2,1)} %pad_maximum_fusion.4), channel_id=1, source_target_pairs={{2,0},{4,2},{6,4},{8,6},{10,8},{12,10},{14,12},{3,1},{5,3},{7,5},{... | collective-permute-start | bytes 3145736 | tf_op jit(solution)/shard_map/ppermute | solution.py:25
  533.7 65.8 %copy-start.7 = (bf16[3,128,2048]{1,2,0:T(8,128)(2,1)S(1)}, bf16[3,128,2048]{1,2,0:T(8,128)(2,1)}, u32[]{:S(2)}) copy-start(bf16[3,128,2048]{1,2,0:T(8,128)(2,1)} %copy.122) | copy-start | bytes 4718596
  609.1 1.6 copy-start.11
  620.6 1.6 copy-start.11
  632.2 1.6 copy-start.11
  643.7 1.6 copy-start.11
  648.6 1.0 copy-start.10
  797.9 19.4 %copy-start.1 = (s32[8,32,3]{1,0,2:T(8,128)S(1)}, s32[8,32,3]{1,0,2:T(8,128)}, u32[]{:S(2)}) copy-start(s32[8,32,3]{1,0,2:T(8,128)} %param.18) | copy-start | bytes 9220
Sparse Core Ops, SparseCore 0:
  10.1 179.1 all-gather.3
  191.5 174.6 all-gather.5
  415.8 152.4 all-reduce.1
  570.2 227.6 all-gather.7
  810.6 6.7 reduce-scatter.1
